TPU v7x, 32 devices: a whole 2x2x4 slice. The times are simulated.
32 devices in a mesh: grp: 2 (over x), row: 16 (over z, y, core).
Axes of the slice: x: 2, y: 2, z: 4, core: 2. Of those that a mesh axis runs over, the one named last changes fastest.
Arguments:
- saved_rows: float32 [32, 512, 32, 128], P(None, None, ('grp', 'row')), may hold values from -3 to 3
- table_order: int32 [32], replicated, may hold values from 0 to 31, each once
- owner_shard: int32 [32, 32, 128, 1], P(None, ('grp', 'row')), may hold values from 0 to 15; in each aligned block of 128 rows (0 to 127, 128 to 255, ..., all dimensions but the last counted through in order) at most 24 rows name the same one
- row_in_shard: int32 [32, 32, 128], P(None, ('grp', 'row')), may hold values from 0 to 1023
- bag_owner: int32 [32, 32, 128], P(None, ('grp', 'row')), may hold values from 0 to 15, never falling along the last dimension, each value on 1 to 32 neighbouring positions
Outputs:
- pooled: float32 [512, 32, 128], P(('grp', 'row'))
Inputs may be any that keep to these rules, and one draw needn't show every extreme that they name: `owner_shard`: among the 128 ids of one table and one device, no shard number occurs more than 24 times, and 24 is reached in some of these blocks. `bag_owner`: never falls along the last dimension; every sample has 1 to 32 ids of each table. `table_order`: each table number once.
All inputs are finite; a program needn't handle non-finite values.
Results may differ from a plain program's by a relative error of at most 0.00007.
Values sent between devices are 32-bit elements; how exact they have to be, the bound alone decides.
A program may use at most 128 MiB of HBM per device.

v0:
```python
import jax
import jax.numpy as jnp
from jax import lax
from jax.sharding import PartitionSpec as P

SAMP_DEV = 16


def fetch_rows(restored, wanted):
    per_group, row_count, columns = restored.shape
    present = wanted >= 0
    safe_rows = jnp.maximum(wanted, 0)
    table_base = (jnp.arange(per_group, dtype=jnp.int32) * row_count).reshape(
        (1,) * (wanted.ndim - 2) + (per_group, 1)
    )
    flat_index = (safe_rows + table_base).reshape(-1)
    fetched = jnp.take(restored.reshape(per_group * row_count, columns), flat_index, axis=0)
    fetched = fetched.reshape(wanted.shape + (columns,))
    return jnp.where(present[..., None], fetched, 0.0)


def body(saved_rows, table_order, owner_shard, row_in_shard, bag_owner):
    groups = lax.axis_size("grp")
    shards = lax.axis_size("row")
    devices = groups * shards
    table_count, saved_depth, _, columns = saved_rows.shape
    per_group = table_count // groups
    row_block = saved_depth // shards
    picker = (table_order[:, None] == jnp.arange(table_count, dtype=jnp.int32)[None, :]).astype(
        jnp.float32
    )
    ordered_rows = jnp.einsum(
        "cu,uqd->cqd",
        picker,
        saved_rows.reshape(table_count, saved_depth, columns),
        precision=lax.Precision.HIGHEST,
    )
    parcel = ordered_rows.reshape(groups, per_group, shards, row_block, columns)
    parcel = jnp.transpose(parcel, (0, 2, 1, 3, 4)).reshape(
        devices, per_group, row_block, 1, columns
    )
    placed = lax.all_to_all(parcel, ("grp", "row"), split_axis=0, concat_axis=3, tiled=True)
    restored = placed.reshape(per_group, row_block * devices, columns)
    ids_count = row_in_shard.shape[2]
    capacity = 3 * ids_count // shards
    target_shard = owner_shard[table_order][:, 0, :, 0]
    local_row = row_in_shard[table_order][:, 0, :]
    sample_of = bag_owner[table_order][:, 0, :]
    matches = (
        target_shard[:, :, None] == jnp.arange(shards, dtype=jnp.int32)[None, None, :]
    ).astype(jnp.int32)
    slot_rank = jnp.sum(jnp.cumsum(matches, axis=1) * matches, axis=2) - 1
    order_pos = jnp.arange(table_count, dtype=jnp.int32)[:, None]
    group_of = order_pos // per_group
    within = order_pos % per_group
    requests = jnp.full((groups, shards, per_group, capacity), -1, jnp.int32)
    requests = requests.at[group_of, target_shard, within, slot_rank].set(local_row)
    returned = lax.all_to_all(
        fetch_rows(
            restored,
            lax.all_to_all(
                requests.reshape(devices, per_group, capacity),
                ("grp", "row"),
                split_axis=0,
                concat_axis=0,
                tiled=True,
            ),
        ),
        ("grp", "row"),
        split_axis=0,
        concat_axis=0,
        tiled=True,
    )
    returned = returned.reshape(groups, shards, per_group, capacity, columns)
    slot_key = target_shard * capacity + slot_rank
    slot_hits = (
        slot_key[:, :, None] == jnp.arange(shards * capacity, dtype=jnp.int32)[None, None, :]
    ).astype(jnp.float32)
    member = (sample_of[:, None, :] == jnp.arange(SAMP_DEV, dtype=jnp.int32)[None, :, None]).astype(
        jnp.float32
    )
    weights = jnp.einsum("csp,cpj->csj", member, slot_hits, precision=lax.Precision.HIGHEST)
    weights = weights.reshape(groups, per_group, SAMP_DEV, shards, capacity)
    pooled = jnp.einsum("gwsrk,grwkd->sgwd", weights, returned, precision=lax.Precision.HIGHEST)
    return pooled.reshape(SAMP_DEV, table_count, columns)


def solution(mesh):
    return jax.shard_map(
        body,
        mesh=mesh,
        in_specs=(
            P(None, None, ("grp", "row"), None),
            P(),
            P(None, ("grp", "row"), None, None),
            P(None, ("grp", "row"), None),
            P(None, ("grp", "row"), None),
        ),
        out_specs=P(("grp", "row"), None, None),
        check_vma=False,
    )
```

profile of v0, /device:TPU:0, one launch (start us, length us, event | category | flops | bytes accessed | tf_op | source)
XLA Modules:
  0.0 455.5 jit_solution(487431897516483985)
XLA Ops:
  0.0 0.7 compare_select_fusion.5
  0.7 0.6 gather_fusion
  1.3 0.1 copy.17
  1.4 3.3 select_reduce_fusion
  4.8 0.1 broadcast_in_dim.33
  4.9 0.1 broadcast_in_dim.31
  5.0 0.7 and_reduce_fusion
  5.7 0.7 multiply_reduce_fusion
  6.4 1.3 gather_fusion.1
  7.7 15.5 %scatter_custom_fusion = s32[12288]{0:T(1024)S(1)} fusion(s32[4096]{0:T(1024)S(1)} %select_bitcast_fusion, s32[4096]{0:T(1024)S(1)} %bitcast.54, s32[]{:T(128)} %constant.57.clone.1), kind=kCustom, calls=%fused_computation.33 | custom fusion | bytes 49156
  23.3 0.2 reshape.221
  23.5 0.8 reshape.294
  24.3 7.5 %all-to-all-start = ((s32[32,1,384]{2,1,0:T(1,128)}), s32[32,1,384]{2,1,0:T(1,128)S(1)}, u32[]{:S(2)}, u32[]{:S(2)}) async-start(s32[32,1,384]{2,1,0:T(1,128)} %reshape.294), calls=%async_computation | async-start | bytes 98304 | tf_op jit(solution)/shard_map/all_to_all | solution.py:61
  31.8 0.7 eq.80
  32.5 15.6 %fusion = f32[2,16,16,32,128]{4,1,3,2,0:T(8,128)} fusion(f32[16,32,128,32]{2,1,0,3:T(8,128)} %bitcast.49, s32[2,16]{1,0:T(2,128)S(1)} %eq.80), kind=kOutput, calls=%fused_computation.5 | convolution fusion | flops 805307392 | bytes 16777344 | tf_op jit(solution)/shard_map/cu,uqd->cqd/dot_general | solution.py:32
  48.1 6.0 %all-to-all-start.1 = ((f32[32,16,32,1,128]{4,1,2,3,0:T(8,128)}), f32[32,16,32,1,128]{4,1,2,3,0:T(8,128)}, u32[]{:S(2)}, u32[]{:S(2)}) async-start(f32[32,16,32,1,128]{4,1,2,3,0:T(8,128)} %bitcast.47), calls=%async_computation.1 | async-start | bytes 16777216 | tf_op jit(solution)/shard_map/all_to_all | solution.py:42
  54.2 0.5 broadcast.261
  54.7 0.8 reduce.4
  55.4 0.2 reshape.295
  55.6 0.2 compare_and_fusion
  55.8 0.2 reshape.224
  56.1 182.6 %all-to-all-done.1 = f32[32,16,32,1,128]{4,1,2,3,0:T(8,128)} async-done(((f32[32,16,32,1,128]{4,1,2,3,0:T(8,128)}), f32[32,16,32,1,128]{4,1,2,3,0:T(8,128)}, u32[]{:S(2)}, u32[]{:S(2)}) %all-to-all-start.1) | async-done | bytes 8388640 | tf_op jit(solution)/shard_map/all_to_all | solution.py:42
  238.7 11.4 %copy.22 = f32[1,16,32,32,1,128]{5,3,2,1,4,0:T(8,128)} copy(f32[1,16,32,32,1,128]{5,1,2,3,4,0:T(8,128)} %bitcast.18) | data formatting | bytes 16777216 | tf_op jit(solution)/shard_map/all_to_all | solution.py:42
  250.2 44.4 %gather_fusion.2 = f32[12288,128]{1,0:T(8,128)} fusion(f32[16384,128]{1,0:T(8,128)} %bitcast.46, s32[12288]{0:T(1024)S(1)} %broadcast_clamp_fusion), kind=kCustom, calls=%fused_computation.2 | custom fusion | bytes 12632064 | tf_op jit(solution)/shard_map/jit(_take)/gather | solution.py:17
  294.5 6.4 %select_select_fusion = f32[32,16,24,128]{3,2,1,0:T(8,128)} fusion(f32[32,16,24,128]{3,2,1,0:T(8,128)} %bitcast.48, pred[32,16,24]{2,1,0:T(8,128)(4,1)S(1)} %get-tuple-element.5, pred[32,16,24]{2,1,0:T(8,128)(4,1)S(1)} %get-tuple-element.7), kind=kLoop, calls=%fused_computation.11 | loop fusion | flops 3145728 | bytes 12607488 | tf_op jit(solution)/shard_map/jit(_where)/select_n | solution.py:19
  300.9 3.8 all-to-all-start.2
  304.7 0.6 gather_fusion.3
  305.3 1.7 fusion.5
  307.0 4.0 reshape.226
  311.0 133.3 %all-to-all-done.2 = f32[32,16,24,128]{3,2,1,0:T(8,128)} async-done(((f32[32,16,24,128]{3,2,1,0:T(8,128)}), f32[32,16,24,128]{3,2,1,0:T(8,128)}, u32[]{:S(2)}, u32[]{:S(2)}) %all-to-all-start.2) | async-done | bytes 6291488 | tf_op jit(solution)/shard_map/all_to_all | solution.py:58
  444.2 10.5 %fusion.3 = f32[2,16,128,16,1]{2,3,4,1,0:T(8,128)S(1)} fusion(f32[2,16,16,24,128]{4,3,2,1,0:T(8,128)} %bitcast.22, f32[2,16,16,16,24]{4,3,2,1,0:T(8,128)} %reshape.226), kind=kOutput, calls=%fused_computation.8 | convolution fusion | flops 301989888 | bytes 7340032 | tf_op jit(solution)/shard_map/gwsrk,grwkd->sgwd/dot_general | solution.py:84
  454.8 0.8 copy.25
  (15 shorter events, 0.2 us)
Async XLA Ops:
  0.0 0.7 copy-start
  24.3 23.9 %all-to-all-start = ((s32[32,1,384]{2,1,0:T(1,128)}), s32[32,1,384]{2,1,0:T(1,128)S(1)}, u32[]{:S(2)}, u32[]{:S(2)}) async-start(s32[32,1,384]{2,1,0:T(1,128)} %reshape.294), calls=%async_computation | async-start | bytes 98304 | tf_op jit(solution)/shard_map/all_to_all | solution.py:61
  48.1 190.6 %all-to-all-start.1 = ((f32[32,16,32,1,128]{4,1,2,3,0:T(8,128)}), f32[32,16,32,1,128]{4,1,2,3,0:T(8,128)}, u32[]{:S(2)}, u32[]{:S(2)}) async-start(f32[32,16,32,1,128]{4,1,2,3,0:T(8,128)} %bitcast.47), calls=%async_computation.1 | async-start | bytes 16777216 | tf_op jit(solution)/shard_map/all_to_all | solution.py:42
  300.9 3.8 copy-start.1
  300.9 143.3 %all-to-all-start.2 = ((f32[32,16,24,128]{3,2,1,0:T(8,128)}), f32[32,16,24,128]{3,2,1,0:T(8,128)}, u32[]{:S(2)}, u32[]{:S(2)}) async-start(f32[32,16,24,128]{3,2,1,0:T(8,128)} %select_select_fusion), calls=%async_computation.2 | async-start | bytes 12582912 | tf_op jit(solution)/shard_map/all_to_all | solution.py:58
where the time goes:
time: 456 us
  waiting for transfers between devices  316 us (69%)
  local copies, waits for them, and re-layouts  81.5 us (18%)
  matrix products  27.8 us (6%)
  starting transfers between devices  17.3 us (4%)
  other arithmetic  12.9 us (3%)
    all_to_all x1, waiting for transfers between devices, body(): lax.all_to_all(parcel, ('grp', 'row'), split_axis=0, concat_axis=3, tiled...  183 us
    all_to_all x1, waiting for transfers between devices, body(): lax.all_to_all(fetch_rows(restored, lax.all_to_all(requests.reshape(devic...  133 us
    gather x1, local copies, waits for them, and re-layouts, fetch_rows(): jnp.take(restored.reshape(per_group * row_count, columns), flat_index, ax...  44.4 us
    unnamed x7, local copies, waits for them, and re-layouts  16.6 us
    dot_general x1, matrix products, body(): jnp.einsum('cu,uqd->cqd', picker, saved_rows.reshape(table_count, saved_d...  15.6 us
    all_to_all x1, local copies, waits for them, and re-layouts, body(): lax.all_to_all(parcel, ('grp', 'row'), split_axis=0, concat_axis=3, tiled...  11.4 us
    dot_general x1, matrix products, body(): jnp.einsum('gwsrk,grwkd->sgwd', weights, returned, precision=lax.Precisio...  10.5 us
  transfers between devices with their start and end apart: 3, of which 2 were waited for; matrix products, arithmetic and copies ran while one was open for 5% of the time, Pallas kernels for 0%

commit v1 on v0

v1 whole, which is shorter than its diff:
```python
import functools

import jax
import jax.numpy as jnp
from jax import lax
from jax.experimental import pallas as pl
from jax.experimental.pallas import tpu as pltpu
from jax.sharding import PartitionSpec as P

SAMP_DEV = 16
MESH = pl.DeviceIdType.MESH
BF16 = jnp.bfloat16


def pool_kernel(groups, shards, order_ref, ids_ref, saved_ref, out_ref,
                rows, split, counts, part, got1, got2, got3, mine, res,
                row_sem, swap_send, swap_recv, send1, recv1, send2, recv2, send3, recv3, last_send, last_recv):
    half, _, depth, columns = rows.shape
    tables = 2 * half
    far = shards // 4
    devices = groups * shards
    assert devices & (devices - 1) == 0
    q_high = depth // 128
    samples = SAMP_DEV
    pair = 2 * samples
    g = lax.axis_index("grp")
    row = lax.axis_index("row")
    core = lax.rem(row, 2)
    m = lax.rem(row // 2, 2)
    a = row // 4
    chip = (g * shards + row) // 2
    flip = 1 - 2 * core

    def place(gg, aa, mm, cc):
        return (gg, (aa * 2 + mm) * 2 + cc)

    sibling = place(g, a, m, 1 - core)
    is0 = 1 - core
    near1 = place(lax.rem(g + is0, 2), a, lax.rem(m + core, 2), core)
    near2 = place(lax.rem(g + core, 2), a, lax.rem(m + is0, 2), core)

    def far_place(d):
        return place(g, lax.rem(a + d, far), m, core)

    barrier = pltpu.get_barrier_semaphore()
    for peer in [sibling, near1, near2] + [far_place(d) for d in range(1, far)]:
        pl.semaphore_signal(barrier, inc=1, device_id=peer, device_id_type=MESH)
    pl.semaphore_wait(barrier, 2 + far)

    def own_rows(t):
        return pltpu.make_async_copy(saved_ref.at[core * half + t], rows.at[t, core], row_sem.at[t])

    def swap_rows(t):
        return pltpu.make_async_remote_copy(
            src_ref=saved_ref.at[(1 - core) * half + t], dst_ref=rows.at[t, core],
            send_sem=swap_send.at[t], recv_sem=swap_recv.at[t], device_id=sibling, device_id_type=MESH)

    def swap_got(t):
        return pltpu.make_async_remote_copy(
            src_ref=saved_ref.at[(1 - core) * half + t], dst_ref=rows.at[t, 1 - core],
            send_sem=swap_send.at[t], recv_sem=swap_recv.at[t], device_id=sibling, device_id_type=MESH)

    def first(t):
        return pltpu.make_async_remote_copy(
            src_ref=part.at[t, 1], dst_ref=got1.at[t], send_sem=send1.at[t], recv_sem=recv1.at[t],
            device_id=near1, device_id_type=MESH)

    def second(t):
        return pltpu.make_async_remote_copy(
            src_ref=part.at[t, 0, 1], dst_ref=got2.at[t], send_sem=send2.at[t], recv_sem=recv2.at[t],
            device_id=near2, device_id_type=MESH)

    def third(t, d):
        return pltpu.make_async_remote_copy(
            src_ref=part.at[t, 0, 0, lax.rem(a + d, far)], dst_ref=got3.at[t, d - 1],
            send_sem=send3.at[t, d - 1], recv_sem=recv3.at[t, d - 1],
            device_id=far_place(d), device_id_type=MESH)

    def start_rows(t, carry):
        own_rows(t).start()
        swap_rows(t).start()
        return carry

    lax.fori_loop(0, half, start_rows, 0)

    key_rows = 2 * q_high * samples
    key_iota = lax.broadcasted_iota(jnp.int32, (key_rows, 128), 0)
    low_iota = lax.broadcasted_iota(jnp.int32, (128, 128), 0)

    def split_rows(t):
        own_rows(t).wait()
        swap_got(t).wait_recv()
        for k in range(2):
            x = rows[t, k]
            high = x.astype(BF16)
            split[k * depth:(k + 1) * depth, 0:columns] = high
            split[k * depth:(k + 1) * depth, columns:] = (x - high.astype(jnp.float32)).astype(BF16)

    def product(t, side):
        u = core * half + t
        per_side = 2 * far * 2

        def one(r, carry):
            c2 = lax.rem(r, 2)
            aa = lax.rem(r // 2, far)
            p2 = r // (2 * far)
            gg = lax.rem(g + is0 * side + core * p2, 2)
            mm = lax.rem(m + core * side + is0 * p2, 2)
            j = gg * shards + (aa * 2 + mm) * 2 + c2
            ids = ids_ref[j, pl.ds(u, 1), :]
            bag = ids_ref[j, pl.ds(tables + u, 1), :]
            dev = ids & (devices - 1)
            q = ids >> (devices.bit_length() - 1)
            key = ((dev & 1) * q_high + (q >> 7)) * samples + bag
            key = jnp.where((dev >> 1) == chip, key, -1)
            low = q & 127
            lhs = jnp.where(key == key_iota, 1.0, 0.0).astype(BF16)
            rhs = jnp.where(low == low_iota, 1.0, 0.0).astype(BF16)
            c = lax.dot_general(lhs, rhs, (((1,), (1,)), ((), ())), preferred_element_type=jnp.float32).astype(BF16)
            at = pl.ds(pl.multiple_of(r * samples, samples), samples)
            for i in range(2 * q_high):
                counts[at, i * 128:(i + 1) * 128] = c[i * samples:(i + 1) * samples]
            return carry

        lax.fori_loop(0, per_side, one, 0, unroll=4)
        for p2 in range(2):
            for_rows = counts[p2 * far * pair:(p2 + 1) * far * pair, :]
            both = jnp.dot(for_rows, split[...], preferred_element_type=jnp.float32)
            part[t, side, p2] = (both[:, :columns] + both[:, columns:]).reshape(far, pair, columns)

    def step(i, carry):
        @pl.when(i < half)
        def _():
            split_rows(i)
            product(i, 1)
            first(i).start()

        @pl.when(jnp.logical_and(i >= 1, i < half + 1))
        def _():
            t = i - 1
            first(t).wait_recv()
            part[t, 0, 1] += got1[t, 1]
            second(t).start()
            part[t, 0, 0] += got1[t, 0]

        @pl.when(jnp.logical_and(i >= 2, i < half + 2))
        def _():
            t = i - 2
            second(t).wait_recv()
            part[t, 0, 0] += got2[t]
            for d in range(1, far):
                third(t, d).start()

        @pl.when(jnp.logical_and(i >= 3, i < half + 3))
        def _():
            t = i - 3
            total = part[t, 0, 0, a]
            for d in range(1, far):
                third(t, d).wait_recv()
                total = total + got3[t, d - 1]
            mine[t] = total

        @pl.when(i < half)
        def _():
            product(i, 0)

        return carry

    lax.fori_loop(0, half + 3, step, 0)

    def hand_over(t, carry):
        res[core * half + t] = mine[t, pl.ds(pl.multiple_of(core * samples, samples), samples), :]
        return carry

    last = pltpu.make_async_remote_copy(
        src_ref=mine.at[:, pl.ds(pl.multiple_of((1 - core) * samples, samples), samples), :],
        dst_ref=res.at[pl.ds(core * half, half)],
        send_sem=last_send, recv_sem=last_recv, device_id=sibling, device_id_type=MESH)
    last.start()
    lax.fori_loop(0, half, hand_over, 0)

    def drain(t, carry):
        swap_rows(t).wait_send()
        first(t).wait_send()
        second(t).wait_send()
        for d in range(1, far):
            third(t, d).wait_send()
        return carry

    lax.fori_loop(0, half, drain, 0)
    last.wait()
    for c in range(tables):
        out_ref[:, c, :] = res[order_ref[c]]


def body(saved_rows, table_order, owner_shard, row_in_shard, bag_owner):
    groups = lax.axis_size("grp")
    shards = lax.axis_size("row")
    devices = groups * shards
    tables, depth, _, columns = saved_rows.shape
    half = tables // 2
    far = shards // 4
    shard_rows = depth * devices // shards
    ids = owner_shard[:, 0, :, 0] * shard_rows + row_in_shard[:, 0, :]
    wanted = lax.all_gather(jnp.concatenate([ids, bag_owner[:, 0, :]], axis=0), ("grp", "row"))
    pair = 2 * SAMP_DEV
    f32 = jnp.float32
    dma = pltpu.SemaphoreType.DMA
    return pl.pallas_call(
        functools.partial(pool_kernel, groups, shards),
        out_shape=jax.ShapeDtypeStruct((SAMP_DEV, tables, columns), f32),
        in_specs=[
            pl.BlockSpec(memory_space=pltpu.SMEM),
            pl.BlockSpec(memory_space=pltpu.VMEM),
            pl.BlockSpec(memory_space=pl.ANY),
        ],
        out_specs=pl.BlockSpec(memory_space=pltpu.VMEM),
        scratch_shapes=[
            pltpu.VMEM((half, 2, depth, columns), f32),
            pltpu.VMEM((2 * depth, 2 * columns), BF16),
            pltpu.VMEM((2 * far * pair, 2 * depth), BF16),
            pltpu.VMEM((half, 2, 2, far, pair, columns), f32),
            pltpu.VMEM((half, 2, far, pair, columns), f32),
            pltpu.VMEM((half, far, pair, columns), f32),
            pltpu.VMEM((half, far - 1, pair, columns), f32),
            pltpu.VMEM((half, pair, columns), f32),
            pltpu.VMEM((tables, SAMP_DEV, columns), f32),
            dma((half,)), dma((half,)), dma((half,)),
            dma((half,)), dma((half,)), dma((half,)), dma((half,)),
            dma((half, far - 1)), dma((half, far - 1)),
            dma, dma,
        ],
        compiler_params=pltpu.CompilerParams(collective_id=0, has_side_effects=True),
    )(table_order, wanted, saved_rows.reshape(tables, depth, columns))


def solution(mesh):
    return jax.shard_map(
        body,
        mesh=mesh,
        in_specs=(
            P(None, None, ("grp", "row"), None),
            P(),
            P(None, ("grp", "row"), None, None),
            P(None, ("grp", "row"), None),
            P(None, ("grp", "row"), None),
        ),
        out_specs=P(("grp", "row"), None, None),
        check_vma=False,
    )
```

time: 456 us -> 150 us (0.33)
  waiting for transfers between devices: 316 us -> 58 us
  local copies, waits for them, and re-layouts: 81.5 us -> 1.67 us
  Pallas kernels: 0 us -> 74.3 us
  matrix products: 27.8 us -> 0 us
  starting transfers between devices: 17.3 us -> 0.01 us
  between operations: 0.15 us -> 13.4 us
  other arithmetic: 12.9 us -> 2.07 us
    all_to_all x3 -> x0, waiting for transfers between devices: 316 us -> none  [the longest x1 183 us: body(): lax.all_to_all(parcel, ('grp', 'row'), split_axis=0, concat_axis=3, tiled...]
    pallas_call x0 -> x1, Pallas kernels: none -> 74.3 us  [body(): pl.pallas_call(functools.partial(pool_kernel, groups, shards), out_shape=...]
    all_gather x0 -> x1, waiting for transfers between devices: none -> 58 us  [body(): lax.all_gather(jnp.concatenate([ids, bag_owner[:, 0, :]], axis=0), ('grp'...]
    gather x5 -> x0, local copies, waits for them, and re-layouts: 46.9 us -> none  [the longest x1 44.4 us: fetch_rows(): jnp.take(restored.reshape(per_group * row_count, columns), flat_index, ax...]
    dot_general x3 -> x0, matrix products: 27.8 us -> none  [the longest x1 15.6 us: body(): jnp.einsum('cu,uqd->cqd', picker, saved_rows.reshape(table_count, saved_d...]
    all_to_all x3 -> x0, starting transfers between devices: 17.3 us -> none  [the longest x1 7.51 us: body(): lax.all_to_all(requests.reshape(devices, per_group, capacity), ('grp', 'r...]
    unnamed x7 -> x1, local copies, waits for them, and re-layouts: 16.6 us -> 1.67 us
    all_to_all x2 -> x0, local copies, waits for them, and re-layouts: 12 us -> none  [the longest x1 11.4 us: body(): lax.all_to_all(parcel, ('grp', 'row'), split_axis=0, concat_axis=3, tiled...]
  transfers between devices with their start and end apart: 3 -> 1, of which waited for: 2 -> 1; matrix products, arithmetic and copies ran while one was open for 5% -> 0% of each run, Pallas kernels for 0% -> 0%
where the time goes in v1:
time: 150 us; the launch traced here: 149 us
  Pallas kernels  74.3 us (50%)
  waiting for transfers between devices  58 us (39%)
  between operations  13.4 us (9%)
  other arithmetic  2.07 us (1%)
  local copies, waits for them, and re-layouts  1.67 us (1%)
    pallas_call x1, Pallas kernels, body(): pl.pallas_call(functools.partial(pool_kernel, groups, shards), out_shape=...  74.3 us
    all_gather x1, waiting for transfers between devices, body(): lax.all_gather(jnp.concatenate([ids, bag_owner[:, 0, :]], axis=0), ('grp'...  58 us
  transfers between devices with their start and end apart: 1, of which 1 were waited for; matrix products, arithmetic and copies ran while one was open for 0% of the time, Pallas kernels for 0%

profile of v1, /device:TPU:0, one launch (start us, length us, event | category | flops | bytes accessed | tf_op | source)
XLA Modules:
  0.0 149.4 jit_solution(12685296222069377154)
XLA Ops:
  6.5 0.0 all-gather.3.cloned.1.call-start
  6.5 0.7 bitcast_add_fusion
  7.3 1.3 pad_add_fusion
  8.6 0.0 all-gather.3.cloned.1.call-update
  8.6 58.0 %all-gather.3.cloned.1.call-done = s32[2048,128]{1,0:T(8,128)} async-done(((s32[64,128]{1,0:T(8,128)}), s32[2048,128]{1,0:T(8,128)}) %all-gather.3.cloned.1.call-update) | async-done | bytes 1048592 | tf_op jit(solution)/shard_map/all_gather | solution.py:205
  66.7 74.3 %shard_map.55 = f32[16,32,128]{2,1,0:T(8,128)} custom-call(s32[32]{0:T(128)} %order_ref.1, s32[32,64,128]{2,1,0:T(8,128)} %bitcast.8, f32[32,512,128]{2,1,0:T(8,128)} %bitcast.7), custom_call_target="tpu_custom_call" | custom-call | tf_op jit(solution)/shard_map/pallas_call | solution.py:209
  140.9 1.7 %copy.8 = f32[16,32,128]{2,1,0:T(8,128)} copy(f32[16,32,128]{2,1,0:T(8,128)} %shard_map.55) | data formatting | bytes 524288
Async XLA Ops:
  6.5 60.1 %all-gather.3.cloned.1.call-start = ((), (), s32[]{:S(2)}) async-start(), calls=%async_computation | async-start | bytes 1081344 | tf_op jit(solution)/shard_map/all_gather | solution.py:205
Sparse Core Ops, SparseCore 0:
  10.2 56.3 all-gather.2

commit v2 on v1

--- a/solution.py
+++ b/solution.py
@@ -12,7 +12,9 @@
 BF16 = jnp.bfloat16
 
 
-def pool_kernel(groups, shards, order_ref, ids_ref, saved_ref, out_ref,
+def pool_kernel(groups, shards, order_ref, own_ref, saved_ref, out_ref,
+                ids, own_sem, ask0_send, ask0_recv, ask3_send, ask3_recv, ask2_send, ask2_recv,
+                ask1_send, ask1_recv, ask12_send, ask12_recv,
                 rows, split, counts, part, got1, got2, got3, mine, res,
                 row_sem, swap_send, swap_recv, send1, recv1, send2, recv2, send3, recv3, last_send, last_recv):
     half, _, depth, columns = rows.shape
@@ -81,7 +83,48 @@
         swap_rows(t).start()
         return carry
 
+    def keep_ids(k):
+        return pltpu.make_async_copy(own_ref.at[core, k], ids.at[k, 0, 0, a, core], own_sem.at[k])
+
+    def ask(src, dst, sends, recvs, peer):
+        return pltpu.make_async_remote_copy(
+            src_ref=src, dst_ref=dst, send_sem=sends, recv_sem=recvs, device_id=peer, device_id_type=MESH)
+
+    def ask0(k):
+        return ask(own_ref.at[1 - core, k], ids.at[k, 0, 0, a, core], ask0_send.at[k], ask0_recv.at[k], sibling)
+
+    def ask3(k, d):
+        return ask(ids.at[k, 0, 0, a], ids.at[k, 0, 0, a],
+                   ask3_send.at[k, d - 1], ask3_recv.at[k, d - 1], far_place(d))
+
+    def ask2(k):
+        return ask(ids.at[k, 0, 0], ids.at[k, 0, 1], ask2_send.at[k], ask2_recv.at[k], near2)
+
+    def ask1(k):
+        return ask(ids.at[k, 0, 0], ids.at[k, 1, 0], ask1_send.at[k], ask1_recv.at[k], near1)
+
+    def ask12(k):
+        return ask(ids.at[k, 0, 1], ids.at[k, 1, 1], ask12_send.at[k], ask12_recv.at[k], near1)
+
+    chunks = ids.shape[0]
+    per_chunk = half // chunks
+    for k in range(chunks):
+        ask0(k).start()
+        keep_ids(k).start()
     lax.fori_loop(0, half, start_rows, 0)
+    for k in range(chunks):
+        keep_ids(k).wait()
+        ask0(k).wait_recv()
+        for d in range(1, far):
+            ask3(k, d).start()
+    for k in range(chunks):
+        for d in range(1, far):
+            ask3(k, d).wait_recv()
+        ask2(k).start()
+        ask1(k).start()
+    for k in range(chunks):
+        ask2(k).wait_recv()
+        ask12(k).start()
 
     key_rows = 2 * q_high * samples
     key_iota = lax.broadcasted_iota(jnp.int32, (key_rows, 128), 0)
@@ -97,20 +140,19 @@
             split[k * depth:(k + 1) * depth, columns:] = (x - high.astype(jnp.float32)).astype(BF16)
 
     def product(t, side):
-        u = core * half + t
         per_side = 2 * far * 2
+        chunk = t // per_chunk
+        slot = lax.rem(t, per_chunk)
 
         def one(r, carry):
             c2 = lax.rem(r, 2)
             aa = lax.rem(r // 2, far)
             p2 = r // (2 * far)
-            gg = lax.rem(g + is0 * side + core * p2, 2)
-            mm = lax.rem(m + core * side + is0 * p2, 2)
-            j = gg * shards + (aa * 2 + mm) * 2 + c2
-            ids = ids_ref[j, pl.ds(u, 1), :]
-            bag = ids_ref[j, pl.ds(tables + u, 1), :]
-            dev = ids & (devices - 1)
-            q = ids >> (devices.bit_length() - 1)
+            block = ids.at[chunk, side, p2, aa, c2]
+            want = block[pl.ds(slot, 1), :]
+            bag = block[pl.ds(per_chunk + slot, 1), :]
+            dev = want & (devices - 1)
+            q = want >> (devices.bit_length() - 1)
             key = ((dev & 1) * q_high + (q >> 7)) * samples + bag
             key = jnp.where((dev >> 1) == chip, key, -1)
             low = q & 127
@@ -131,6 +173,11 @@
     def step(i, carry):
         @pl.when(i < half)
         def _():
+            @pl.when(lax.rem(i, per_chunk) == 0)
+            def _():
+                ask1(i // per_chunk).wait_recv()
+                ask12(i // per_chunk).wait_recv()
+
             split_rows(i)
             product(i, 1)
             first(i).start()
@@ -188,6 +235,13 @@
         return carry
 
     lax.fori_loop(0, half, drain, 0)
+    for k in range(chunks):
+        ask0(k).wait_send()
+        for d in range(1, far):
+            ask3(k, d).wait_send()
+        ask2(k).wait_send()
+        ask1(k).wait_send()
+        ask12(k).wait_send()
     last.wait()
     for c in range(tables):
         out_ref[:, c, :] = res[order_ref[c]]
@@ -202,7 +256,10 @@
     far = shards // 4
     shard_rows = depth * devices // shards
     ids = owner_shard[:, 0, :, 0] * shard_rows + row_in_shard[:, 0, :]
-    wanted = lax.all_gather(jnp.concatenate([ids, bag_owner[:, 0, :]], axis=0), ("grp", "row"))
+    chunks = max(1, half // 4)
+    per_chunk = half // chunks
+    cut = (2, chunks, per_chunk, ids.shape[-1])
+    wanted = jnp.concatenate([ids.reshape(cut), bag_owner[:, 0, :].reshape(cut)], axis=2)
     pair = 2 * SAMP_DEV
     f32 = jnp.float32
     dma = pltpu.SemaphoreType.DMA
@@ -216,6 +273,10 @@
         ],
         out_specs=pl.BlockSpec(memory_space=pltpu.VMEM),
         scratch_shapes=[
+            pltpu.VMEM((chunks, 2, 2, far, 2, 2 * per_chunk, ids.shape[-1]), jnp.int32),
+            dma((chunks,)), dma((chunks,)), dma((chunks,)),
+            dma((chunks, far - 1)), dma((chunks, far - 1)),
+            dma((chunks,)), dma((chunks,)), dma((chunks,)), dma((chunks,)), dma((chunks,)), dma((chunks,)),
             pltpu.VMEM((half, 2, depth, columns), f32),
             pltpu.VMEM((2 * depth, 2 * columns), BF16),
             pltpu.VMEM((2 * far * pair, 2 * depth), BF16),

time: 150 us -> 92.1 us (0.61)
  waiting for transfers between devices: 58 us -> 0 us
  between operations: 13.4 us -> 0.01 us
  Pallas kernels: 74.3 us -> 87.2 us
    all_gather x1 -> x0, waiting for transfers between devices: 58 us -> none  [body(): lax.all_gather(jnp.concatenate([ids, bag_owner[:, 0, :]], axis=0), ('grp'...]
    pallas_call x1, Pallas kernels: 74.3 us -> 87.2 us  [body(): pl.pallas_call(functools.partial(pool_kernel, groups, shards), out_shape=...]
  transfers between devices with their start and end apart: 1 -> 0, of which waited for: 1 -> 0; matrix products, arithmetic and copies ran while one was open for 0% -> 0% of each run, Pallas kernels for 0% -> 0%
where the time goes in v2:
time: 92.1 us; the launch traced here: 91.7 us
  Pallas kernels  87.2 us (95%)
  other arithmetic  2.8 us (3%)
  local copies, waits for them, and re-layouts  1.67 us (2%)
    pallas_call x1, Pallas kernels, body(): pl.pallas_call(functools.partial(pool_kernel, groups, shards), out_shape=...  87.2 us

profile of v2, /device:TPU:0, one launch (start us, length us, event | category | flops | bytes accessed | tf_op | source)
XLA Modules:
  0.0 91.7 jit_solution(8486366410582867003)
XLA Ops:
  0.0 0.7 broadcast_multiply_fusion
  0.7 0.7 add.4
  1.5 1.3 %pad_add_fusion.own_ref = s32[2,4,8,128]{3,2,1,0:T(8,128)} fusion(s32[2,4,4,128]{3,2,1,0:T(4,128)} %bitcast.7, s32[2,4,4,128]{3,2,1,0:T(4,128)S(1)} %add.4), kind=kLoop, calls=%fused_computation | loop fusion | flops 8192 | bytes 65536 | tf_op jit(solution)/shard_map/concatenate | solution.py:262
  2.8 87.2 %shard_map.55 = f32[16,32,128]{2,1,0:T(8,128)} custom-call(s32[32]{0:T(128)} %order_ref.1, s32[2,4,8,128]{3,2,1,0:T(8,128)} %pad_add_fusion.own_ref, f32[32,512,128]{2,1,0:T(8,128)} %bitcast.4), custom_call_target="tpu_custom_call" | custom-call | tf_op jit(solution)/shard_map/pallas_call | solution.py:266
  90.0 1.7 %copy.7 = f32[16,32,128]{2,1,0:T(8,128)} copy(f32[16,32,128]{2,1,0:T(8,128)} %shard_map.55) | data formatting | bytes 524288

commit v3 on v2

--- a/solution.py
+++ b/solution.py
@@ -8,6 +8,7 @@
 from jax.sharding import PartitionSpec as P
 
 SAMP_DEV = 16
+LAG = 2
 MESH = pl.DeviceIdType.MESH
 BF16 = jnp.bfloat16
 
@@ -117,14 +118,19 @@
         ask0(k).wait_recv()
         for d in range(1, far):
             ask3(k, d).start()
-    for k in range(chunks):
+
+    def ask_near(k):
         for d in range(1, far):
             ask3(k, d).wait_recv()
         ask2(k).start()
         ask1(k).start()
-    for k in range(chunks):
+
+    def ask_last(k):
         ask2(k).wait_recv()
         ask12(k).start()
+
+    ask_near(0)
+    ask_last(0)
 
     key_rows = 2 * q_high * samples
     key_iota = lax.broadcasted_iota(jnp.int32, (key_rows, 128), 0)
@@ -171,6 +177,12 @@
             part[t, side, p2] = (both[:, :columns] + both[:, columns:]).reshape(far, pair, columns)
 
     def step(i, carry):
+        ahead = i // per_chunk + 1
+        for turn, stage in enumerate((ask_near, ask_last)):
+            @pl.when(jnp.logical_and(lax.rem(i, per_chunk) == turn, ahead < chunks))
+            def _(stage=stage):
+                stage(ahead)
+
         @pl.when(i < half)
         def _():
             @pl.when(lax.rem(i, per_chunk) == 0)
@@ -182,25 +194,25 @@
             product(i, 1)
             first(i).start()
 
-        @pl.when(jnp.logical_and(i >= 1, i < half + 1))
-        def _():
-            t = i - 1
+        @pl.when(jnp.logical_and(i >= LAG, i < half + LAG))
+        def _():
+            t = i - LAG
             first(t).wait_recv()
             part[t, 0, 1] += got1[t, 1]
             second(t).start()
             part[t, 0, 0] += got1[t, 0]
 
-        @pl.when(jnp.logical_and(i >= 2, i < half + 2))
-        def _():
-            t = i - 2
+        @pl.when(jnp.logical_and(i >= 2 * LAG, i < half + 2 * LAG))
+        def _():
+            t = i - 2 * LAG
             second(t).wait_recv()
             part[t, 0, 0] += got2[t]
             for d in range(1, far):
                 third(t, d).start()
 
-        @pl.when(jnp.logical_and(i >= 3, i < half + 3))
-        def _():
-            t = i - 3
+        @pl.when(jnp.logical_and(i >= 3 * LAG, i < half + 3 * LAG))
+        def _():
+            t = i - 3 * LAG
             total = part[t, 0, 0, a]
             for d in range(1, far):
                 third(t, d).wait_recv()
@@ -213,7 +225,7 @@
 
         return carry
 
-    lax.fori_loop(0, half + 3, step, 0)
+    lax.fori_loop(0, half + 3 * LAG, step, 0)
 
     def hand_over(t, carry):
         res[core * half + t] = mine[t, pl.ds(pl.multiple_of(core * samples, samples), samples), :]

time: 92.1 us -> 77.7 us (0.84)
  Pallas kernels: 87.2 us -> 72.8 us
    pallas_call x1, Pallas kernels: 87.2 us -> 72.8 us  [body(): pl.pallas_call(functools.partial(pool_kernel, groups, shards), out_shape=...]
where the time goes in v3:
time: 77.7 us; the launch traced here: 77.3 us
  Pallas kernels  72.8 us (94%)
  other arithmetic  2.8 us (4%)
  local copies, waits for them, and re-layouts  1.67 us (2%)
    pallas_call x1, Pallas kernels, body(): pl.pallas_call(functools.partial(pool_kernel, groups, shards), out_shape=...  72.8 us
    unnamed x1, local copies, waits for them, and re-layouts  1.67 us

profile of v3, /device:TPU:0, one launch (start us, length us, event | category | flops | bytes accessed | tf_op | source)
XLA Modules:
  0.0 77.3 jit_solution(8388726275721966270)
XLA Ops:
  0.0 0.7 broadcast_multiply_fusion
  0.7 0.7 add.4
  1.5 1.3 %pad_add_fusion.own_ref = s32[2,4,8,128]{3,2,1,0:T(8,128)} fusion(s32[2,4,4,128]{3,2,1,0:T(4,128)} %bitcast.7, s32[2,4,4,128]{3,2,1,0:T(4,128)S(1)} %add.4), kind=kLoop, calls=%fused_computation | loop fusion | flops 8192 | bytes 65536 | tf_op jit(solution)/shard_map/concatenate | solution.py:274
  2.8 72.8 %shard_map.55 = f32[16,32,128]{2,1,0:T(8,128)} custom-call(s32[32]{0:T(128)} %order_ref.1, s32[2,4,8,128]{3,2,1,0:T(8,128)} %pad_add_fusion.own_ref, f32[32,512,128]{2,1,0:T(8,128)} %bitcast.4), custom_call_target="tpu_custom_call" | custom-call | tf_op jit(solution)/shard_map/pallas_call | solution.py:278
  75.6 1.7 %copy.7 = f32[16,32,128]{2,1,0:T(8,128)} copy(f32[16,32,128]{2,1,0:T(8,128)} %shard_map.55) | data formatting | bytes 524288

commit v4 on v3

--- a/solution.py
+++ b/solution.py
@@ -8,6 +8,7 @@
 from jax.sharding import PartitionSpec as P
 
 SAMP_DEV = 16
+UNROLL = 16
 LAG = 2
 MESH = pl.DeviceIdType.MESH
 BF16 = jnp.bfloat16
@@ -145,16 +146,16 @@
             split[k * depth:(k + 1) * depth, 0:columns] = high
             split[k * depth:(k + 1) * depth, columns:] = (x - high.astype(jnp.float32)).astype(BF16)
 
-    def product(t, side):
-        per_side = 2 * far * 2
+    def product(t):
+        every = 2 * 2 * far * 2
         chunk = t // per_chunk
         slot = lax.rem(t, per_chunk)
 
         def one(r, carry):
             c2 = lax.rem(r, 2)
             aa = lax.rem(r // 2, far)
-            p2 = r // (2 * far)
-            block = ids.at[chunk, side, p2, aa, c2]
+            p2 = lax.rem(r // (2 * far), 2)
+            block = ids.at[chunk, r // (4 * far), p2, aa, c2]
             want = block[pl.ds(slot, 1), :]
             bag = block[pl.ds(per_chunk + slot, 1), :]
             dev = want & (devices - 1)
@@ -170,11 +171,9 @@
                 counts[at, i * 128:(i + 1) * 128] = c[i * samples:(i + 1) * samples]
             return carry
 
-        lax.fori_loop(0, per_side, one, 0, unroll=4)
-        for p2 in range(2):
-            for_rows = counts[p2 * far * pair:(p2 + 1) * far * pair, :]
-            both = jnp.dot(for_rows, split[...], preferred_element_type=jnp.float32)
-            part[t, side, p2] = (both[:, :columns] + both[:, columns:]).reshape(far, pair, columns)
+        lax.fori_loop(0, every, one, 0, unroll=UNROLL)
+        both = jnp.dot(counts[...], split[...], preferred_element_type=jnp.float32)
+        part[t] = (both[:, :columns] + both[:, columns:]).reshape(2, 2, far, pair, columns)
 
     def step(i, carry):
         ahead = i // per_chunk + 1
@@ -191,7 +190,7 @@
                 ask12(i // per_chunk).wait_recv()
 
             split_rows(i)
-            product(i, 1)
+            product(i)
             first(i).start()
 
         @pl.when(jnp.logical_and(i >= LAG, i < half + LAG))
@@ -218,10 +217,6 @@
                 third(t, d).wait_recv()
                 total = total + got3[t, d - 1]
             mine[t] = total
-
-        @pl.when(i < half)
-        def _():
-            product(i, 0)
 
         return carry
 
@@ -291,7 +286,7 @@
             dma((chunks,)), dma((chunks,)), dma((chunks,)), dma((chunks,)), dma((chunks,)), dma((chunks,)),
             pltpu.VMEM((half, 2, depth, columns), f32),
             pltpu.VMEM((2 * depth, 2 * columns), BF16),
-            pltpu.VMEM((2 * far * pair, 2 * depth), BF16),
+            pltpu.VMEM((4 * far * pair, 2 * depth), BF16),
             pltpu.VMEM((half, 2, 2, far, pair, columns), f32),
             pltpu.VMEM((half, 2, far, pair, columns), f32),
             pltpu.VMEM((half, far, pair, columns), f32),

time: 77.7 us -> 74.4 us (0.958)
  Pallas kernels: 72.8 us -> 69.5 us
    pallas_call x1, Pallas kernels: 72.8 us -> 69.5 us  [body(): pl.pallas_call(functools.partial(pool_kernel, groups, shards), out_shape=...]
where the time goes in v4:
time: 74.4 us; the launch traced here: 74 us
  Pallas kernels  69.5 us (93%)
  other arithmetic  2.8 us (4%)
  local copies, waits for them, and re-layouts  1.67 us (2%)
    pallas_call x1, Pallas kernels, body(): pl.pallas_call(functools.partial(pool_kernel, groups, shards), out_shape=...  69.5 us
    unnamed x1, local copies, waits for them, and re-layouts  1.67 us

profile of v4, /device:TPU:0, one launch (start us, length us, event | category | flops | bytes accessed | tf_op | source)
XLA Modules:
  0.0 74.0 jit_solution(5619136621254348219)
XLA Ops:
  0.0 0.7 broadcast_multiply_fusion
  0.7 0.7 add.4
  1.5 1.3 %pad_add_fusion.own_ref = s32[2,4,8,128]{3,2,1,0:T(8,128)} fusion(s32[2,4,4,128]{3,2,1,0:T(4,128)} %bitcast.7, s32[2,4,4,128]{3,2,1,0:T(4,128)S(1)} %add.4), kind=kLoop, calls=%fused_computation | loop fusion | flops 8192 | bytes 65536 | tf_op jit(solution)/shard_map/concatenate | solution.py:269
  2.8 69.5 %shard_map.55 = f32[16,32,128]{2,1,0:T(8,128)} custom-call(s32[32]{0:T(128)} %order_ref.1, s32[2,4,8,128]{3,2,1,0:T(8,128)} %pad_add_fusion.own_ref, f32[32,512,128]{2,1,0:T(8,128)} %bitcast.4), custom_call_target="tpu_custom_call" | custom-call | tf_op jit(solution)/shard_map/pallas_call | solution.py:273
  72.3 1.7 %copy.7 = f32[16,32,128]{2,1,0:T(8,128)} copy(f32[16,32,128]{2,1,0:T(8,128)} %shard_map.55) | data formatting | bytes 524288

commit v5 on v4

--- a/solution.py
+++ b/solution.py
@@ -14,8 +14,8 @@
 BF16 = jnp.bfloat16
 
 
-def pool_kernel(groups, shards, order_ref, own_ref, saved_ref, out_ref,
-                ids, own_sem, ask0_send, ask0_recv, ask3_send, ask3_recv, ask2_send, ask2_recv,
+def pool_kernel(groups, shards, order_ref, owner_ref, local_ref, bag_ref, saved_ref, out_ref,
+                own_ref, ids, own_sem, ask0_send, ask0_recv, ask3_send, ask3_recv, ask4_send, ask4_recv, ask2_send, ask2_recv,
                 ask1_send, ask1_recv, ask12_send, ask12_recv,
                 rows, split, counts, part, got1, got2, got3, mine, res,
                 row_sem, swap_send, swap_recv, send1, recv1, send2, recv2, send3, recv3, last_send, last_recv):
@@ -43,13 +43,24 @@
     near1 = place(lax.rem(g + is0, 2), a, lax.rem(m + core, 2), core)
     near2 = place(lax.rem(g + core, 2), a, lax.rem(m + is0, 2), core)
 
-    def far_place(d):
-        return place(g, lax.rem(a + d, far), m, core)
+    diagonal = place(1 - g, a, 1 - m, core)
+
+    def far_place(d, cc):
+        return place(g, lax.rem(a + d, far), m, cc)
+
+    shard_rows = depth * devices // shards
+    chunks = ids.shape[0]
+    per_chunk = half // chunks
+    for t in range(tables):
+        h, k, slot = t // half, t % half // per_chunk, t % per_chunk
+        own_ref[h, k, slot:slot + 1, :] = owner_ref[t] * shard_rows + local_ref[t]
+        own_ref[h, k, per_chunk + slot:per_chunk + slot + 1, :] = bag_ref[t]
 
     barrier = pltpu.get_barrier_semaphore()
-    for peer in [sibling, near1, near2] + [far_place(d) for d in range(1, far)]:
+    peers = [sibling, near1, near2, diagonal] + [far_place(d, cc) for d in range(1, far) for cc in (core, 1 - core)]
+    for peer in peers:
         pl.semaphore_signal(barrier, inc=1, device_id=peer, device_id_type=MESH)
-    pl.semaphore_wait(barrier, 2 + far)
+    pl.semaphore_wait(barrier, len(peers))
 
     def own_rows(t):
         return pltpu.make_async_copy(saved_ref.at[core * half + t], rows.at[t, core], row_sem.at[t])
@@ -78,7 +89,7 @@
         return pltpu.make_async_remote_copy(
             src_ref=part.at[t, 0, 0, lax.rem(a + d, far)], dst_ref=got3.at[t, d - 1],
             send_sem=send3.at[t, d - 1], recv_sem=recv3.at[t, d - 1],
-            device_id=far_place(d), device_id_type=MESH)
+            device_id=far_place(d, core), device_id_type=MESH)
 
     def start_rows(t, carry):
         own_rows(t).start()
@@ -96,8 +107,12 @@
         return ask(own_ref.at[1 - core, k], ids.at[k, 0, 0, a, core], ask0_send.at[k], ask0_recv.at[k], sibling)
 
     def ask3(k, d):
-        return ask(ids.at[k, 0, 0, a], ids.at[k, 0, 0, a],
-                   ask3_send.at[k, d - 1], ask3_recv.at[k, d - 1], far_place(d))
+        return ask(own_ref.at[core, k], ids.at[k, 0, 0, a, core],
+                   ask3_send.at[k, d - 1], ask3_recv.at[k, d - 1], far_place(d, core))
+
+    def ask4(k, d):
+        return ask(own_ref.at[1 - core, k], ids.at[k, 0, 0, a, core],
+                   ask4_send.at[k, d - 1], ask4_recv.at[k, d - 1], far_place(d, 1 - core))
 
     def ask2(k):
         return ask(ids.at[k, 0, 0], ids.at[k, 0, 1], ask2_send.at[k], ask2_recv.at[k], near2)
@@ -106,32 +121,27 @@
         return ask(ids.at[k, 0, 0], ids.at[k, 1, 0], ask1_send.at[k], ask1_recv.at[k], near1)
 
     def ask12(k):
-        return ask(ids.at[k, 0, 1], ids.at[k, 1, 1], ask12_send.at[k], ask12_recv.at[k], near1)
-
-    chunks = ids.shape[0]
-    per_chunk = half // chunks
+        return ask(ids.at[k, 0, 0], ids.at[k, 1, 1], ask12_send.at[k], ask12_recv.at[k], diagonal)
+
     for k in range(chunks):
+        for d in range(1, far):
+            ask3(k, d).start()
+            ask4(k, d).start()
         ask0(k).start()
         keep_ids(k).start()
     lax.fori_loop(0, half, start_rows, 0)
-    for k in range(chunks):
+
+    def ask_near(k):
         keep_ids(k).wait()
         ask0(k).wait_recv()
         for d in range(1, far):
-            ask3(k, d).start()
-
-    def ask_near(k):
-        for d in range(1, far):
             ask3(k, d).wait_recv()
+            ask4(k, d).wait_recv()
+        ask12(k).start()
         ask2(k).start()
         ask1(k).start()
 
-    def ask_last(k):
-        ask2(k).wait_recv()
-        ask12(k).start()
-
     ask_near(0)
-    ask_last(0)
 
     key_rows = 2 * q_high * samples
     key_iota = lax.broadcasted_iota(jnp.int32, (key_rows, 128), 0)
@@ -177,16 +187,16 @@
 
     def step(i, carry):
         ahead = i // per_chunk + 1
-        for turn, stage in enumerate((ask_near, ask_last)):
-            @pl.when(jnp.logical_and(lax.rem(i, per_chunk) == turn, ahead < chunks))
-            def _(stage=stage):
-                stage(ahead)
+        @pl.when(jnp.logical_and(lax.rem(i, per_chunk) == 0, ahead < chunks))
+        def _():
+            ask_near(ahead)
 
         @pl.when(i < half)
         def _():
             @pl.when(lax.rem(i, per_chunk) == 0)
             def _():
                 ask1(i // per_chunk).wait_recv()
+                ask2(i // per_chunk).wait_recv()
                 ask12(i // per_chunk).wait_recv()
 
             split_rows(i)
@@ -246,6 +256,7 @@
         ask0(k).wait_send()
         for d in range(1, far):
             ask3(k, d).wait_send()
+            ask4(k, d).wait_send()
         ask2(k).wait_send()
         ask1(k).wait_send()
         ask12(k).wait_send()
@@ -261,12 +272,9 @@
     tables, depth, _, columns = saved_rows.shape
     half = tables // 2
     far = shards // 4
-    shard_rows = depth * devices // shards
-    ids = owner_shard[:, 0, :, 0] * shard_rows + row_in_shard[:, 0, :]
     chunks = max(1, half // 4)
     per_chunk = half // chunks
-    cut = (2, chunks, per_chunk, ids.shape[-1])
-    wanted = jnp.concatenate([ids.reshape(cut), bag_owner[:, 0, :].reshape(cut)], axis=2)
+    width = row_in_shard.shape[-1]
     pair = 2 * SAMP_DEV
     f32 = jnp.float32
     dma = pltpu.SemaphoreType.DMA
@@ -276,13 +284,16 @@
         in_specs=[
             pl.BlockSpec(memory_space=pltpu.SMEM),
             pl.BlockSpec(memory_space=pltpu.VMEM),
+            pl.BlockSpec(memory_space=pltpu.VMEM),
+            pl.BlockSpec(memory_space=pltpu.VMEM),
             pl.BlockSpec(memory_space=pl.ANY),
         ],
         out_specs=pl.BlockSpec(memory_space=pltpu.VMEM),
         scratch_shapes=[
-            pltpu.VMEM((chunks, 2, 2, far, 2, 2 * per_chunk, ids.shape[-1]), jnp.int32),
+            pltpu.VMEM((2, chunks, 2 * per_chunk, width), jnp.int32),
+            pltpu.VMEM((chunks, 2, 2, far, 2, 2 * per_chunk, width), jnp.int32),
             dma((chunks,)), dma((chunks,)), dma((chunks,)),
-            dma((chunks, far - 1)), dma((chunks, far - 1)),
+            dma((chunks, far - 1)), dma((chunks, far - 1)), dma((chunks, far - 1)), dma((chunks, far - 1)),
             dma((chunks,)), dma((chunks,)), dma((chunks,)), dma((chunks,)), dma((chunks,)), dma((chunks,)),
             pltpu.VMEM((half, 2, depth, columns), f32),
             pltpu.VMEM((2 * depth, 2 * columns), BF16),
@@ -299,7 +310,7 @@
             dma, dma,
         ],
         compiler_params=pltpu.CompilerParams(collective_id=0, has_side_effects=True),
-    )(table_order, wanted, saved_rows.reshape(tables, depth, columns))
+    )(table_order, owner_shard[..., 0], row_in_shard, bag_owner, saved_rows.reshape(tables, depth, columns))
 
 
 def solution(mesh):

time: 74.4 us -> 68.2 us (0.917)
  Pallas kernels: 69.5 us -> 66.3 us
  other arithmetic: 2.8 us -> 0 us
    pallas_call x1, Pallas kernels: 69.5 us -> 66.3 us  [body(): pl.pallas_call(functools.partial(pool_kernel, groups, shards), out_shape=...]
    concatenate x1 -> x0, other arithmetic: 1.34 us -> none  [body(): jnp.concatenate([ids.reshape(cut), bag_owner[:, 0, :].reshape(cut)], axis=2)]
where the time goes in v5:
time: 68.2 us; the launch traced here: 67.9 us
  Pallas kernels  66.3 us (97%)
  local copies, waits for them, and re-layouts  1.67 us (2%)
    pallas_call x1, Pallas kernels, body(): pl.pallas_call(functools.partial(pool_kernel, groups, shards), out_shape=...  66.3 us
    unnamed x1, local copies, waits for them, and re-layouts  1.67 us

profile of v5, /device:TPU:0, one launch (start us, length us, event | category | flops | bytes accessed | tf_op | source)
XLA Modules:
  0.0 67.9 jit_solution(1572001739956811951)
XLA Ops:
  0.0 66.3 %shard_map.55 = f32[16,32,128]{2,1,0:T(8,128)} custom-call(s32[32]{0:T(128)} %order_ref.1, s32[32,1,128]{2,1,0:T(1,128)} %bitcast.3, s32[32,1,128]{2,1,0:T(1,128)} %local_ref.1, s32[32,1,128]{2,1,0:T(1,128)} %bag_ref.1, f32[32,512,128]{2,1,0:T(8,128)} %bitcast.2), custom_call_target="tpu_custom_call" | custom-call | tf_op jit(solution)/shard_map/pallas_call | solution.py:281
  66.3 1.7 %copy.7 = f32[16,32,128]{2,1,0:T(8,128)} copy(f32[16,32,128]{2,1,0:T(8,128)} %shard_map.55) | data formatting | bytes 524288
